TPU v7x, 32 devices: a whole 2x2x4 slice. The times are simulated.
32 devices in a mesh: region: 4 (over z), enc: 8 (over y, x, core).
Axes of the slice: x: 2, y: 2, z: 4, core: 2. Of those that a mesh axis runs over, the one named last changes fastest.
Arguments:
- pixels: bfloat16 [256, 48, 4096], P(('region', 'enc')), may hold values from -6 to 6
- feature_grad: bfloat16 [256, 96, 4096], P(('region', 'enc')), may hold values from -0.0046691895 to 0.0046691895
- tissue_count: int32 [32], P(('region', 'enc')), may hold values from 1 to 8, as said below
- stem_weight: bfloat16 [96, 48], replicated, may hold values from -0.875 to 0.875
- stem_gain: float32 [96], replicated, may hold values from 0.5 to 1.5
- stem_shift: float32 [96], replicated, may hold values from -3 to 3
- depth_kernel: float32 [96, 49], replicated, may hold values from -0.875 to 0.875
- block_gain: float32 [96], replicated, may hold values from 0.5 to 1.5
- expand_weight: bfloat16 [384, 96], replicated, may hold values from -0.625 to 0.625
- expand_bias: float32 [384], replicated, may hold values from -3 to 3
- reduce_weight: bfloat16 [96, 384], replicated, may hold values from -0.3125 to 0.3125
- layer_scale: float32 [96], replicated, may hold values from 0.5 to 1.5
Outputs:
- features: bfloat16 [256, 96, 4096], P(('region', 'enc'))
- grad_stem: float32 [96, 48], replicated
- grad_gain: float32 [96], replicated
- grad_shift: float32 [96], replicated
- grad_kernel: float32 [96, 49], replicated
- grad_norm: float32 [96], replicated
- grad_expand: float32 [384, 96], replicated
- grad_bias: float32 [384], replicated
- grad_reduce: float32 [96, 384], replicated
- grad_scale: float32 [96], replicated
Inputs may be any that keep to these rules, and one draw needn't show every extreme that they name: `tissue_count`: the tissue tiles of a device fill its first slots; the other slots are unused.
All inputs are finite; a program needn't handle non-finite values.
Results may differ from a plain program's by a relative error of at most 0.015.
Values may be sent and summed in bfloat16 or wider, within the bound.
A program may use at most 256 MiB of HBM per device.

v0:
```python
from functools import partial

import jax
import jax.numpy as jnp
import numpy as np
from jax import lax
from jax.experimental import pallas as pl
from jax.experimental.pallas import tpu as pltpu
from jax.sharding import PartitionSpec as P

SIDE = 64
KSIZE = 7
EPS = 1e-06
LANES = 128
CHUNK = 512
PAD = 2
BLOCKS = 10
EXTRA = 16

f32 = jnp.float32
bf16 = jnp.bfloat16


def dot(a, b, dims=((1,), (0,))):
    return lax.dot_general(a, b, (dims, ((), ())), preferred_element_type=f32)


def wide(value, times):
    return jnp.concatenate([value] * times, axis=1)


def fold(value):
    total = value[:, :LANES]
    for at in range(LANES, value.shape[1], LANES):
        total = total + value[:, at : at + LANES]
    return total


def unit(values):
    centre = jnp.mean(values, axis=0, keepdims=True)
    shifted = values - centre
    spread = jnp.mean(jnp.square(shifted), axis=0, keepdims=True)
    scale = lax.rsqrt(spread + EPS)
    return shifted * scale, scale


def unit_back(grad, hat, scale):
    first = jnp.mean(grad, axis=0, keepdims=True)
    second = jnp.mean(grad * hat, axis=0, keepdims=True)
    return scale * (grad - first - hat * second)


def gelu_both(x):
    decay = jnp.exp(x * x * -0.5)
    t = 1.0 / (1.0 + jnp.abs(x) * (0.3275911 * 0.7071067811865476))
    poly = t * (
        0.5 * 0.254829592
        + t
        * (
            0.5 * -0.284496736
            + t * (0.5 * 1.421413741 + t * (0.5 * -1.453152027 + t * (0.5 * 1.061405429)))
        )
    )
    tail = poly * decay
    cdf = jnp.where(x >= 0, 1.0 - tail, tail)
    return x * cdf, cdf + x * (decay * 0.3989422804014327)


def body(
    count_ref, pix_ref, grad_ref, ws_ref, par_ref, we_ref, wet_ref, wr_ref, wrt_ref, taps_ref,
    back_ref, feat_ref, dws_ref, dvec_ref, dwe_ref, dwr_ref, dk_ref, base_s, mix_s, ex_s, dh_s,
    hid_s, de_s,
):
    phase = pl.program_id(0)
    slot = pl.program_id(1)
    slots = pl.num_programs(1)
    live = slot < count_ref[0]
    channels, area = grad_ref.shape[1:]
    pairs = area // LANES
    per = CHUNK // LANES
    chunks = area // CHUNK
    hidden = we_ref.shape[0]
    rows = base_s.shape[1] // channels

    row_at = lax.broadcasted_iota(jnp.int32, (SIDE, LANES), 0)
    lane_at = lax.broadcasted_iota(jnp.int32, (SIDE, LANES), 1) % SIDE
    near = jnp.abs(row_at - lane_at) <= KSIZE // 2
    near_mirrored = jnp.abs(SIDE - 1 - row_at - lane_at) <= KSIZE // 2
    row_all = lax.broadcasted_iota(jnp.int32, (LANES, LANES), 0)
    lane_all = lax.broadcasted_iota(jnp.int32, (LANES, LANES), 1)
    same = row_all // SIDE == lane_all // SIDE
    mirror = (same & (row_all % SIDE + lane_all % SIDE == SIDE - 1)).astype(f32).astype(bf16)

    def read(ref, chunk):
        return jnp.concatenate(
            [
                ref[PAD + chunk * per + at, pl.ds(slot, channels, stride=rows), :]
                for at in range(per)
            ],
            axis=1,
        )

    def write(ref, chunk, value):
        for at in range(per):
            ref[PAD + chunk * per + at, pl.ds(slot, channels, stride=rows), :] = value[
                :, at * LANES : (at + 1) * LANES
            ]

    def param(at):
        return wide(par_ref[at], per)

    def toeplitz(ref, c):
        blocks = []
        for m in range(BLOCKS):
            row = jnp.broadcast_to(ref[c, m : m + 1, :], (SIDE, LANES))
            turned = pltpu.roll(row, 0, 1, stride=1, stride_axis=0)
            blocks.append(jnp.where(near, turned, 0.0).astype(bf16))
        return jnp.concatenate(blocks, axis=0)

    def gathered(ref, c):
        at = pl.multiple_of(c * rows, rows)
        full = ref[:, pl.ds(at, rows), :]
        even = full.reshape((pairs + 2 * PAD) * rows, LANES).astype(bf16)
        odd = full[1 : pairs + 3].reshape((pairs + 2) * rows, LANES).astype(bf16)
        size = pairs * rows
        return jnp.concatenate(
            [
                even[:size],
                odd[:size],
                even[2 * rows : 2 * rows + size],
                odd[2 * rows : 2 * rows + size],
                even[4 * rows : 4 * rows + size],
            ],
            axis=1,
        )

    @pl.when((phase == 0) & (slot == 0))
    def _():
        base_s[...] = jnp.zeros(base_s.shape, f32)
        mix_s[...] = jnp.zeros(mix_s.shape, f32)
        dws_ref[...] = jnp.zeros(dws_ref.shape, f32)
        dvec_ref[...] = jnp.zeros(dvec_ref.shape, f32)
        dwe_ref[...] = jnp.zeros(dwe_ref.shape, f32)
        dwr_ref[...] = jnp.zeros(dwr_ref.shape, f32)

    @pl.when((phase == 0) & live)
    def _():
        @pl.loop(0, chunks)
        def _(chunk):
            at = pl.multiple_of(chunk * CHUNK, CHUNK)
            out = dot(ws_ref[...], pix_ref[0, :, pl.ds(at, CHUNK)])
            hat, _ = unit(out)
            base = (hat * param(0) + param(1)).astype(bf16).astype(f32)
            write(base_s, chunk, base)

    @pl.when((phase == 1) & (slot == 0))
    def _():
        @pl.loop(0, channels)
        def _(c):
            out = dot(gathered(base_s, c), toeplitz(taps_ref, c))
            at = pl.multiple_of(c * rows, rows)
            mix_s[PAD : PAD + pairs, pl.ds(at, rows), :] = out.reshape(pairs, rows, LANES)

    @pl.when((phase == 1) & live)
    def _():
        @pl.loop(0, chunks)
        def _(chunk):
            at = pl.multiple_of(chunk * CHUNK, CHUNK)
            hat, scale = unit(read(mix_s, chunk))
            normed = (hat * param(2)).astype(bf16)
            normed = jnp.concatenate([normed, jnp.ones((EXTRA, CHUNK), bf16)], axis=0)
            grad = grad_ref[0, :, pl.ds(at, CHUNK)]
            ex_s[...] = dot(we_ref[...], normed)
            dh_s[...] = dot(wrt_ref[...], (grad.astype(f32) * param(3)).astype(bf16))
            for h in range(0, hidden, 16):
                act, slope = gelu_both(ex_s[h : h + 16, :])
                hid_s[h : h + 16, :] = act.astype(bf16)
                de_s[h : h + 16, :] = (slope * dh_s[h : h + 16, :]).astype(bf16)
            reduced = dot(wr_ref[...], hid_s[...])
            feat_ref[0, :, pl.ds(at, CHUNK)] = (
                read(base_s, chunk) + param(3) * reduced
            ).astype(bf16)
            dwr_ref[...] += dot(grad, hid_s[...], ((1,), (1,)))
            dwe_ref[...] += dot(de_s[...], normed, ((1,), (1,)))
            dn = dot(wet_ref[...], de_s[...])
            dvec_ref[2] += fold(dn * hat)
            write(mix_s, chunk, unit_back(dn * param(2), hat, scale))

    @pl.when((phase == 1) & jnp.logical_not(live))
    def _():
        feat_ref[...] = jnp.zeros(feat_ref.shape, bf16)

    @pl.when((phase == 2) & (slot == 0))
    def _():
        @pl.loop(0, channels)
        def _(c):
            at = pl.multiple_of(c * rows, rows)
            grad = mix_s[PAD : PAD + pairs, pl.ds(at, rows), :]
            grad = grad.reshape(pairs * rows, LANES).astype(bf16)
            grad = dot(grad, mirror).astype(bf16)
            cross = dot(grad, gathered(base_s, c), ((0,), (0,)))
            for r in range(2):
                for k in range(BLOCKS // 2):
                    part = cross[r * SIDE : (r + 1) * SIDE, k * LANES : (k + 1) * LANES]
                    part = pltpu.roll(
                        jnp.where(near_mirrored, part, 0.0), 0, 1, stride=1, stride_axis=0
                    )
                    dk_ref[c, r * 5 + k : r * 5 + k + 1, :] = jnp.sum(
                        part, axis=0, keepdims=True
                    )
            out = dot(gathered(mix_s, c), toeplitz(back_ref, c))
            mix_s[PAD : PAD + pairs, pl.ds(at, rows), :] = out.reshape(pairs, rows, LANES)

    @pl.when((phase == 2) & live)
    def _():
        @pl.loop(0, chunks)
        def _(chunk):
            at = pl.multiple_of(chunk * CHUNK, CHUNK)
            pix = pix_ref[0, :, pl.ds(at, CHUNK)]
            hat, scale = unit(dot(ws_ref[...], pix))
            dbase = grad_ref[0, :, pl.ds(at, CHUNK)].astype(f32) + read(mix_s, chunk)
            dvec_ref[0] += fold(dbase * hat)
            dvec_ref[1] += fold(dbase)
            dstem = unit_back(dbase * param(0), hat, scale).astype(bf16)
            dws_ref[...] += dot(dstem, pix, ((1,), (1,)))


def tap_places():
    half = KSIZE // 2
    place = np.zeros((KSIZE * KSIZE, 16, LANES), np.float32)
    pick = np.zeros((BLOCKS, LANES, KSIZE * KSIZE), np.float32)
    for m in range(BLOCKS):
        for r in range(2):
            a = m - 2 * PAD - r
            if abs(a) > half:
                continue
            for b in range(-half, half + 1):
                tap = (a + half) * KSIZE + b + half
                place[tap, m, (r * SIDE - b) % LANES] = 1.0
                k, rr = divmod(m, 2)
                pick[r * 5 + k, (rr * SIDE + b + SIDE - 1) % LANES, tap] = 1.0
    return place.reshape(KSIZE * KSIZE, -1), pick.reshape(-1, KSIZE * KSIZE)


def encode_slots(pixels, feature_grad, count, weights):
    (ws, stem_gain, stem_shift, kernel, block_gain, we, bias, wr, layer_scale) = weights
    slots, patch, area = pixels.shape
    channels = ws.shape[0]
    hidden = we.shape[0]
    pairs = area // LANES
    place, pick = tap_places()
    exact = lax.Precision.HIGHEST
    taps = jnp.dot(kernel, place, precision=exact).reshape(channels, 16, LANES)
    back = jnp.dot(kernel[:, ::-1], place, precision=exact).reshape(channels, 16, LANES)
    params = jnp.stack([stem_gain, stem_shift, block_gain, layer_scale])
    params = jnp.broadcast_to(params[:, :, None], (4, channels, LANES))
    high = lax.reduce_precision(bias, 8, 7)
    middle = lax.reduce_precision(bias - high, 8, 7)
    low = bias - high - middle
    extra = jnp.stack([high, middle, low], axis=1).astype(bf16)
    we_all = jnp.concatenate(
        [we, extra, jnp.zeros((hidden, EXTRA - extra.shape[1]), bf16)], axis=1
    )

    def pix_at(phase, slot, count):
        last = count[0] - 1
        return (jnp.where(phase == 1, last, jnp.minimum(slot, last)), 0, 0)

    def grad_at(phase, slot, count):
        return (jnp.where(phase == 0, 0, jnp.minimum(slot, count[0] - 1)), 0, 0)

    def feat_at(phase, slot, count):
        return (jnp.where(phase == 0, 0, jnp.where(phase == 1, slot, slots - 1)), 0, 0)

    def whole(shape):
        return pl.BlockSpec(shape, lambda phase, slot, count: (0,) * len(shape))

    consts = (ws, params, we_all, we.T, wr, wr.T, taps, back)
    sums = [
        (channels, patch),
        (3, channels, LANES),
        (hidden, channels + EXTRA),
        (channels, hidden),
        (channels, 16, LANES),
    ]
    outs = pl.pallas_call(
        body,
        grid_spec=pltpu.PrefetchScalarGridSpec(
            num_scalar_prefetch=1,
            grid=(3, slots),
            in_specs=[
                pl.BlockSpec((1, patch, area), pix_at),
                pl.BlockSpec((1, channels, area), grad_at),
            ]
            + [whole(item.shape) for item in consts],
            out_specs=[pl.BlockSpec((1, channels, area), feat_at)] + [whole(s) for s in sums],
            scratch_shapes=[
                pltpu.VMEM((pairs + 2 * PAD, channels * slots, LANES), f32),
                pltpu.VMEM((pairs + 2 * PAD, channels * slots, LANES), f32),
                pltpu.VMEM((hidden, CHUNK), f32),
                pltpu.VMEM((hidden, CHUNK), f32),
                pltpu.VMEM((hidden, CHUNK), bf16),
                pltpu.VMEM((hidden, CHUNK), bf16),
            ],
        ),
        out_shape=[jax.ShapeDtypeStruct((slots, channels, area), bf16)]
        + [jax.ShapeDtypeStruct(s, f32) for s in sums],
        compiler_params=pltpu.CompilerParams(
            dimension_semantics=("arbitrary", "arbitrary"), vmem_limit_bytes=60 * 2**20
        ),
    )(count, pixels, feature_grad, *consts)
    features, dws, dvec, dwe, dwr, dk = outs
    dvec = jnp.sum(dvec, axis=2)
    dk = jnp.dot(dk[:, :BLOCKS].reshape(channels, -1), pick, precision=exact)
    totals = (
        dws,
        dvec[0],
        dvec[1],
        dk,
        dvec[2],
        dwe[:, :channels],
        dwe[:, channels],
        dwr * layer_scale[:, None],
        jnp.sum(dwr * wr.astype(f32), axis=1),
    )
    return features, totals


def on_device(pixels, feature_grad, tissue_count, *weights):
    features, totals = encode_slots(pixels, feature_grad, tissue_count, weights)
    shapes = [item.shape for item in totals]
    flat = jnp.concatenate([item.reshape(-1) for item in totals])
    flat = lax.psum(flat, ("region", "enc"))
    summed = []
    at = 0
    for shape in shapes:
        size = int(np.prod(shape))
        summed.append(flat[at : at + size].reshape(shape))
        at += size
    return (features, *summed)


def solution(mesh):
    return jax.shard_map(
        on_device,
        mesh=mesh,
        in_specs=(
            P(("region", "enc"), None, None),
            P(("region", "enc"), None, None),
            P(("region", "enc")),
        )
        + (P(),) * 9,
        out_specs=(P(("region", "enc"), None, None),) + (P(),) * 9,
        check_vma=False,
    )
```

profile of v0, /device:TPU:1, one launch (start us, length us, event | category | flops | bytes accessed | tf_op | source)
XLA Modules:
  0.0 402.9 jit_solution(5972974119120726737)
XLA Ops:
  7.2 0.0 copy-start.2
  7.2 0.0 copy-start.3
  7.2 0.0 copy-start.4
  7.2 0.0 copy-start.5
  7.2 0.0 all-reduce.2.cloned.1.call-start
  7.9 0.7 fusion
  8.6 1.4 copy.32.ws_ref
  10.0 0.8 rev.3
  10.8 0.1 stack.39
  10.9 0.1 stack.38
  11.0 0.1 stack.37
  11.1 1.0 copy.27
  12.1 1.6 copy.31
  13.8 1.8 convolution_bitcast_fusion.1
  15.6 1.8 convolution_bitcast_fusion
  17.5 1.0 copy.40
  18.5 1.0 copy.39
  19.5 0.0 copy-done.2
  19.5 0.0 copy-done.3
  19.5 0.0 copy-done.4
  19.5 0.0 copy-done.5
  19.6 0.9 concatenate.7.we_ref
  20.4 0.8 broadcast_in_dim.4.par_ref
  21.2 156.4 %shard_map.213 = (bf16[8,96,4096]{2,1,0:T(8,128)(2,1)}, f32[96,48]{1,0:T(8,128)}, f32[3,96,128]{2,1,0:T(8,128)}, f32[384,112]{1,0:T(8,128)}, f32[96,384]{1,0:T(8,128)}, /*index=5*/f32[96,16,128]{2,1,0:T(8,128)}) custom-call(s32[1]{0:T(128)S(6)} %copy.42.count_ref, bf16[8,48,4096]{2,1,0:T(8,128)(2,1)} %pix_ref.1, bf16[8,96,4096]{2,1,0:T(8,128)(2,1)} %grad_ref.1, ...), custom_call_target="tpu_custom_call" | custom-call | tf_op jit(solution)/shard_map/pallas_call | solution.py:286
  177.6 1.1 reduce_sum.18
  178.7 1.2 slice_reduce_fusion
  179.9 0.9 reshape.73
  180.7 1.1 reshape.76
  181.8 0.0 copy-done
  181.8 1.1 multiply_reduce_fusion
  182.9 1.4 copy.33
  184.3 1.2 fusion.3
  185.6 0.2 reshape.75
  185.7 7.4 %concatenate.8 = f32[83808]{0:T(1024)} concatenate(f32[4608]{0:T(1024)S(1)} %reshape.73, f32[96]{0:T(128)S(1)} %get-tuple-element.42, f32[96]{0:T(128)S(1)} %get-tuple-element.41, f32[4704]{0:T(1024)S(1)} %reshape.75, f32[96]{0:T(128)S(1)} %get-tuple-element.40, f32[36864]{0:T(1024)S(1)} %reshape.76, f32[384]{0:T(512)S(1)} %slice_reduce_fusion, f32[36864]{0:T(1024)S(1)} %reshape.77, ...), dimensions={0} | concatenate | bytes 670464 | tf_op jit(solution)/shard_map/concatenate | solution.py:332
  193.1 0.0 all-reduce.2.cloned.1.call-update
  193.2 194.5 %all-reduce.2.cloned.1.call-done = f32[83808]{0:T(1024)} async-done(((f32[83808]{0:T(1024)}), f32[83808]{0:T(1024)}) %all-reduce.2.cloned.1.call-update) | async-done | bytes 335248 | tf_op jit(solution)/shard_map/psum | solution.py:333
  387.7 1.0 fusion.2
  388.7 0.7 reshape.81
  389.4 0.7 slice.76
  390.1 0.1 reshape.78
  390.2 0.7 copy.35
  390.9 0.8 slice.79
  391.7 0.2 reshape.79
  391.9 0.7 copy.36
  392.6 0.1 reshape.80
  392.7 0.8 copy.37
  393.5 1.2 slice.82
  394.7 1.3 fusion.1
  (7 shorter events, 0.1 us)
Async XLA Ops:
  7.2 12.3 %copy-start.2 = (f32[96]{0:T(128)S(1)}, f32[96]{0:T(128)}, u32[]{:S(2)}) copy-start(f32[96]{0:T(128)} %param.25) | copy-start | bytes 1156
  7.2 12.3 %copy-start.3 = (f32[96]{0:T(128)S(1)}, f32[96]{0:T(128)}, u32[]{:S(2)}) copy-start(f32[96]{0:T(128)} %param.21) | copy-start | bytes 1156
  7.2 12.3 %copy-start.4 = (f32[96]{0:T(128)S(1)}, f32[96]{0:T(128)}, u32[]{:S(2)}) copy-start(f32[96]{0:T(128)} %param.19) | copy-start | bytes 1156
  7.2 12.3 %copy-start.5 = (f32[96]{0:T(128)S(1)}, f32[96]{0:T(128)}, u32[]{:S(2)}) copy-start(f32[96]{0:T(128)} %param.18) | copy-start | bytes 1156
  7.2 380.5 %all-reduce.2.cloned.1.call-start = ((), (), s32[]{:S(2)}) async-start(), calls=%async_computation | async-start | bytes 671744 | tf_op jit(solution)/shard_map/psum | solution.py:333
  20.4 161.4 %copy-start = (bf16[96,384]{1,0:T(8,128)(2,1)S(1)}, bf16[96,384]{1,0:T(8,128)(2,1)}, u32[]{:S(2)}) copy-start(bf16[96,384]{1,0:T(8,128)(2,1)} %wr_ref.1) | copy-start | bytes 221188
  21.2 163.1 %copy-start.1 = (f32[1280,49]{1,0:T(8,128)S(1)}, f32[1280,49]{1,0:T(8,128)}, u32[]{:S(2)}) copy-start(f32[1280,49]{1,0:T(8,128)} %constant.9.clone) | copy-start | bytes 752644
Sparse Core Ops, SparseCore 0:
  193.3 194.3 all-reduce.1
where the time goes:
time: 403 us
  waiting for transfers between devices  195 us (48%)
  Pallas kernels  156 us (39%)
  local copies, waits for them, and re-layouts  29.3 us (7%)
  between operations  14.9 us (4%)
  matrix products  4.91 us (1%)
    psum x1, waiting for transfers between devices, on_device(): flat = lax.psum(flat, ('region', 'enc'))  195 us
    pallas_call x1, Pallas kernels, encode_slots(): pl.pallas_call(body, grid_spec=pltpu.PrefetchScalarGridSpec(num_scalar_pr...  156 us
    unnamed x20, local copies, waits for them, and re-layouts  8.28 us
  transfers between devices with their start and end apart: 1, of which 1 were waited for; matrix products, arithmetic and copies ran while one was open for 0% of the time, Pallas kernels for 0%

commit v1 on v0

--- a/solution.py
+++ b/solution.py
@@ -1,5 +1,3 @@
-from functools import partial
-
 import jax
 import jax.numpy as jnp
 import numpy as np
@@ -15,7 +13,8 @@
 CHUNK = 512
 PAD = 2
 BLOCKS = 10
-EXTRA = 16
+EXACT = lax.Precision.HIGHEST
+MESH = pl.DeviceIdType.MESH
 
 f32 = jnp.float32
 bf16 = jnp.bfloat16
@@ -67,9 +66,10 @@
 
 
 def body(
-    count_ref, pix_ref, grad_ref, ws_ref, par_ref, we_ref, wet_ref, wr_ref, wrt_ref, taps_ref,
-    back_ref, feat_ref, dws_ref, dvec_ref, dwe_ref, dwr_ref, dk_ref, base_s, mix_s, ex_s, dh_s,
-    hid_s, de_s,
+    count_ref, pix_ref, grad_ref, ws_ref, gain_ref, shift_ref, norm_ref, scale_ref, kernel_ref,
+    we_in_ref, bias_ref, wr_ref, place_ref, place_back_ref, pick_ref, feat_ref, sums_ref, base_s,
+    mix_s, ex_s, dh_s, hid_s, de_s, par_ref, we_ref, wet_ref, wrt_ref, taps_ref, back_ref,
+    dws_ref, dvec_ref, dwe_ref, dwr_ref, dk_ref,
 ):
     phase = pl.program_id(0)
     slot = pl.program_id(1)
@@ -142,10 +142,31 @@
         dvec_ref[...] = jnp.zeros(dvec_ref.shape, f32)
         dwe_ref[...] = jnp.zeros(dwe_ref.shape, f32)
         dwr_ref[...] = jnp.zeros(dwr_ref.shape, f32)
+        for at, ref in enumerate((gain_ref, shift_ref, norm_ref, scale_ref)):
+            par_ref[at] = jnp.transpose(jnp.broadcast_to(ref[...], (LANES, channels)))
+        kernel = kernel_ref[...].astype(bf16)
+        for m in range(BLOCKS):
+            taps_ref[:, m, :] = dot(kernel, place_ref[m])
+            back_ref[:, m, :] = dot(kernel, place_back_ref[m])
+        weight = we_in_ref[...].astype(f32)
+        wet_ref[...] = jnp.transpose(weight).astype(bf16)
+        wrt_ref[...] = jnp.transpose(wr_ref[...].astype(f32)).astype(bf16)
+        bias = jnp.transpose(jnp.broadcast_to(bias_ref[...], (LANES, hidden)))
+        high = bias.astype(bf16).astype(f32)
+        middle = (bias - high).astype(bf16).astype(f32)
+        low = bias - high - middle
+        lane = lax.broadcasted_iota(jnp.int32, (hidden, LANES), 1)
+        extra = jnp.where(
+            lane == channels,
+            high,
+            jnp.where(lane == channels + 1, middle, jnp.where(lane == channels + 2, low, 0.0)),
+        )
+        we_ref[...] = extra.astype(bf16)
+        we_ref[:, :channels] = we_in_ref[...]
 
     @pl.when((phase == 0) & live)
     def _():
-        @pl.loop(0, chunks)
+        @pl.loop(0, chunks, unroll=2)
         def _(chunk):
             at = pl.multiple_of(chunk * CHUNK, CHUNK)
             out = dot(ws_ref[...], pix_ref[0, :, pl.ds(at, CHUNK)])
@@ -155,7 +176,7 @@
 
     @pl.when((phase == 1) & (slot == 0))
     def _():
-        @pl.loop(0, channels)
+        @pl.loop(0, channels, unroll=4)
         def _(c):
             out = dot(gathered(base_s, c), toeplitz(taps_ref, c))
             at = pl.multiple_of(c * rows, rows)
@@ -163,12 +184,12 @@
 
     @pl.when((phase == 1) & live)
     def _():
-        @pl.loop(0, chunks)
+        @pl.loop(0, chunks, unroll=2)
         def _(chunk):
             at = pl.multiple_of(chunk * CHUNK, CHUNK)
             hat, scale = unit(read(mix_s, chunk))
             normed = (hat * param(2)).astype(bf16)
-            normed = jnp.concatenate([normed, jnp.ones((EXTRA, CHUNK), bf16)], axis=0)
+            normed = jnp.concatenate([normed, jnp.ones((LANES - channels, CHUNK), bf16)], axis=0)
             grad = grad_ref[0, :, pl.ds(at, CHUNK)]
             ex_s[...] = dot(we_ref[...], normed)
             dh_s[...] = dot(wrt_ref[...], (grad.astype(f32) * param(3)).astype(bf16))
@@ -192,7 +213,7 @@
 
     @pl.when((phase == 2) & (slot == 0))
     def _():
-        @pl.loop(0, channels)
+        @pl.loop(0, channels, unroll=4)
         def _(c):
             at = pl.multiple_of(c * rows, rows)
             grad = mix_s[PAD : PAD + pairs, pl.ds(at, rows), :]
@@ -213,7 +234,7 @@
 
     @pl.when((phase == 2) & live)
     def _():
-        @pl.loop(0, chunks)
+        @pl.loop(0, chunks, unroll=2)
         def _(chunk):
             at = pl.multiple_of(chunk * CHUNK, CHUNK)
             pix = pix_ref[0, :, pl.ds(at, CHUNK)]
@@ -222,13 +243,42 @@
             dvec_ref[0] += fold(dbase * hat)
             dvec_ref[1] += fold(dbase)
             dstem = unit_back(dbase * param(0), hat, scale).astype(bf16)
-            dws_ref[...] += dot(dstem, pix, ((1,), (1,)))
-
-
-def tap_places():
+            dws_ref[:, : pix.shape[0]] += dot(dstem, pix, ((1,), (1,)))
+
+    @pl.when((phase == 2) & (slot == slots - 1))
+    def _():
+        mixed = dws_ref[...]
+        for at in range(BLOCKS):
+            mixed += lax.dot_general(
+                dk_ref[:, at, :], pick_ref[at], (((1,), (0,)), ((), ())), precision=EXACT,
+                preferred_element_type=f32,
+            )
+        products = dwr_ref[...]
+        singles = [jnp.sum(dvec_ref[at], axis=1, keepdims=True) for at in range(3)]
+        singles.append(jnp.sum(products * wr_ref[...].astype(f32), axis=1, keepdims=True))
+        lane = lax.broadcasted_iota(jnp.int32, (channels, LANES), 1)
+        start = first_single(pix_ref.shape[1])
+        for at, single in enumerate(singles):
+            mixed = jnp.where(lane == start + at, single, mixed)
+        sums_ref[:channels] = mixed
+        sums_ref[channels : channels + hidden] = dwe_ref[...]
+        top = channels + hidden
+        for at in range(hidden // LANES):
+            sums_ref[top : top + channels] = products[:, at * LANES : (at + 1) * LANES] * par_ref[3]
+            top += channels
+        if top < sums_ref.shape[0]:
+            sums_ref[top:] = jnp.zeros((sums_ref.shape[0] - top, LANES), f32)
+
+
+def first_single(patch):
+    return patch + KSIZE * KSIZE
+
+
+def tap_places(patch):
     half = KSIZE // 2
-    place = np.zeros((KSIZE * KSIZE, 16, LANES), np.float32)
-    pick = np.zeros((BLOCKS, LANES, KSIZE * KSIZE), np.float32)
+    taps = KSIZE * KSIZE
+    place = np.zeros((BLOCKS, taps, LANES), np.float32)
+    pick = np.zeros((BLOCKS, LANES, LANES), np.float32)
     for m in range(BLOCKS):
         for r in range(2):
             a = m - 2 * PAD - r
@@ -236,31 +286,21 @@
                 continue
             for b in range(-half, half + 1):
                 tap = (a + half) * KSIZE + b + half
-                place[tap, m, (r * SIDE - b) % LANES] = 1.0
+                place[m, tap, (r * SIDE - b) % LANES] = 1.0
                 k, rr = divmod(m, 2)
-                pick[r * 5 + k, (rr * SIDE + b + SIDE - 1) % LANES, tap] = 1.0
-    return place.reshape(KSIZE * KSIZE, -1), pick.reshape(-1, KSIZE * KSIZE)
-
-
-def encode_slots(pixels, feature_grad, count, weights):
+                pick[r * 5 + k, (rr * SIDE + b + SIDE - 1) % LANES, patch + tap] = 1.0
+    return place, pick
+
+
+def encode_slots(pixels, feature_grad, count, weights, share=1):
     (ws, stem_gain, stem_shift, kernel, block_gain, we, bias, wr, layer_scale) = weights
     slots, patch, area = pixels.shape
     channels = ws.shape[0]
     hidden = we.shape[0]
     pairs = area // LANES
-    place, pick = tap_places()
-    exact = lax.Precision.HIGHEST
-    taps = jnp.dot(kernel, place, precision=exact).reshape(channels, 16, LANES)
-    back = jnp.dot(kernel[:, ::-1], place, precision=exact).reshape(channels, 16, LANES)
-    params = jnp.stack([stem_gain, stem_shift, block_gain, layer_scale])
-    params = jnp.broadcast_to(params[:, :, None], (4, channels, LANES))
-    high = lax.reduce_precision(bias, 8, 7)
-    middle = lax.reduce_precision(bias - high, 8, 7)
-    low = bias - high - middle
-    extra = jnp.stack([high, middle, low], axis=1).astype(bf16)
-    we_all = jnp.concatenate(
-        [we, extra, jnp.zeros((hidden, EXTRA - extra.shape[1]), bf16)], axis=1
-    )
+    place, pick = tap_places(patch)
+    total = channels + hidden + channels * (hidden // LANES)
+    total = -(-total // (8 * share)) * 8 * share
 
     def pix_at(phase, slot, count):
         last = count[0] - 1
@@ -275,15 +315,12 @@
     def whole(shape):
         return pl.BlockSpec(shape, lambda phase, slot, count: (0,) * len(shape))
 
-    consts = (ws, params, we_all, we.T, wr, wr.T, taps, back)
-    sums = [
-        (channels, patch),
-        (3, channels, LANES),
-        (hidden, channels + EXTRA),
-        (channels, hidden),
-        (channels, 16, LANES),
-    ]
-    outs = pl.pallas_call(
+    consts = (
+        ws, stem_gain[None], stem_shift[None], block_gain[None], layer_scale[None], kernel, we,
+        bias[None], wr, jnp.asarray(place, bf16), jnp.asarray(place[:, ::-1], bf16),
+        jnp.asarray(pick),
+    )
+    return pl.pallas_call(
         body,
         grid_spec=pltpu.PrefetchScalarGridSpec(
             num_scalar_prefetch=1,
@@ -293,7 +330,7 @@
                 pl.BlockSpec((1, channels, area), grad_at),
             ]
             + [whole(item.shape) for item in consts],
-            out_specs=[pl.BlockSpec((1, channels, area), feat_at)] + [whole(s) for s in sums],
+            out_specs=[pl.BlockSpec((1, channels, area), feat_at), whole((total, LANES))],
             scratch_shapes=[
                 pltpu.VMEM((pairs + 2 * PAD, channels * slots, LANES), f32),
                 pltpu.VMEM((pairs + 2 * PAD, channels * slots, LANES), f32),
@@ -301,43 +338,138 @@
                 pltpu.VMEM((hidden, CHUNK), f32),
                 pltpu.VMEM((hidden, CHUNK), bf16),
                 pltpu.VMEM((hidden, CHUNK), bf16),
+                pltpu.VMEM((4, channels, LANES), f32),
+                pltpu.VMEM((hidden, LANES), bf16),
+                pltpu.VMEM((channels, hidden), bf16),
+                pltpu.VMEM((hidden, channels), bf16),
+                pltpu.VMEM((channels, 16, LANES), f32),
+                pltpu.VMEM((channels, 16, LANES), f32),
+                pltpu.VMEM((channels, LANES), f32),
+                pltpu.VMEM((3, channels, LANES), f32),
+                pltpu.VMEM((hidden, LANES), f32),
+                pltpu.VMEM((channels, hidden), f32),
+                pltpu.VMEM((channels, 16, LANES), f32),
             ],
         ),
-        out_shape=[jax.ShapeDtypeStruct((slots, channels, area), bf16)]
-        + [jax.ShapeDtypeStruct(s, f32) for s in sums],
+        out_shape=[
+            jax.ShapeDtypeStruct((slots, channels, area), bf16),
+            jax.ShapeDtypeStruct((total, LANES), f32),
+        ],
         compiler_params=pltpu.CompilerParams(
             dimension_semantics=("arbitrary", "arbitrary"), vmem_limit_bytes=60 * 2**20
         ),
     )(count, pixels, feature_grad, *consts)
-    features, dws, dvec, dwe, dwr, dk = outs
-    dvec = jnp.sum(dvec, axis=2)
-    dk = jnp.dot(dk[:, :BLOCKS].reshape(channels, -1), pick, precision=exact)
-    totals = (
-        dws,
-        dvec[0],
-        dvec[1],
-        dk,
-        dvec[2],
-        dwe[:, :channels],
-        dwe[:, channels],
-        dwr * layer_scale[:, None],
-        jnp.sum(dwr * wr.astype(f32), axis=1),
+
+
+def add_up(
+    sums_ref, stem_ref, gain_ref, shift_ref, kernel_ref, norm_ref, expand_ref, bias_ref, reduce_ref,
+    scale_ref, land_e, land_r, part, middle, full, out_sems, in_sems,
+):
+    count_e = lax.axis_size("enc")
+    count_r = lax.axis_size("region")
+    me_e = lax.axis_index("enc")
+    me_r = lax.axis_index("region")
+    barrier = pltpu.get_barrier_semaphore()
+    for d in range(1, count_e):
+        pl.semaphore_signal(
+            barrier, 1, device_id={"enc": lax.rem(me_e + d, count_e)}, device_id_type=MESH
+        )
+    for d in range(1, count_r):
+        pl.semaphore_signal(
+            barrier, 1, device_id={"region": lax.rem(me_r + d, count_r)}, device_id_type=MESH
+        )
+    pl.semaphore_wait(barrier, count_e + count_r - 2)
+    size_e = part.shape[0]
+    size_r = land_r.shape[1]
+    sems = iter(range(2 * (count_e + count_r - 2)))
+
+    def block(index, size):
+        return pl.ds(pl.multiple_of(index * size, 8), size)
+
+    def exchange(axis, count, me, source, target):
+        copies = []
+        for d in range(1, count):
+            peer = lax.rem(me + d, count)
+            sem = next(sems)
+            copy = pltpu.make_async_remote_copy(
+                src_ref=source(peer), dst_ref=target(d), send_sem=out_sems.at[sem],
+                recv_sem=in_sems.at[sem], device_id={axis: peer}, device_id_type=MESH,
+            )
+            copy.start()
+            copies.append(copy)
+        for copy in copies:
+            copy.wait()
+
+    exchange(
+        "enc", count_e, me_e, lambda peer: sums_ref.at[block(peer, size_e)],
+        lambda d: land_e.at[d - 1],
     )
-    return features, totals
+    value = sums_ref[block(me_e, size_e)]
+    for d in range(1, count_e):
+        value += land_e[d - 1]
+    part[...] = value
+    exchange(
+        "region", count_r, me_r, lambda peer: part.at[block(peer, size_r)],
+        lambda d: land_r.at[d - 1],
+    )
+    value = part[block(me_r, size_r)]
+    for d in range(1, count_r):
+        value += land_r[d - 1]
+    middle[block(me_r, size_r)] = value
+    mine = middle.at[block(me_r, size_r)]
+    exchange("region", count_r, me_r, lambda peer: mine, lambda d: mine)
+    full[block(me_e, size_e)] = middle[...]
+    own = full.at[block(me_e, size_e)]
+    exchange("enc", count_e, me_e, lambda peer: own, lambda d: own)
+
+    channels, patch = stem_ref.shape
+    hidden = expand_ref.shape[0]
+    mixed = full[:channels]
+    stem_ref[...] = mixed[:, :patch]
+    start = first_single(patch)
+    kernel_ref[...] = mixed[:, patch:start]
+    turned = jnp.transpose(mixed)
+    for at, ref in enumerate((gain_ref, shift_ref, norm_ref, scale_ref)):
+        ref[...] = turned[start + at : start + at + 1]
+    wide_rows = full[channels : channels + hidden]
+    expand_ref[...] = wide_rows[:, :channels]
+    bias_ref[...] = jnp.transpose(wide_rows)[channels : channels + 1]
+    top = channels + hidden
+    for at in range(hidden // LANES):
+        reduce_ref[:, at * LANES : (at + 1) * LANES] = full[top : top + channels]
+        top += channels
+
+
+def summed_over_devices(sums, weights):
+    count_e = lax.axis_size("enc")
+    count_r = lax.axis_size("region")
+    size_e = sums.shape[0] // count_e
+    size_r = size_e // count_r
+    copies = 2 * (count_e + count_r - 2)
+    shapes = [item.shape if item.ndim == 2 else (1, item.shape[0]) for item in weights]
+    outs = pl.pallas_call(
+        add_up,
+        in_specs=[pl.BlockSpec(memory_space=pltpu.VMEM)],
+        out_specs=[pl.BlockSpec(memory_space=pltpu.VMEM)] * len(shapes),
+        out_shape=[jax.ShapeDtypeStruct(shape, f32) for shape in shapes],
+        scratch_shapes=[
+            pltpu.VMEM((count_e - 1, size_e, LANES), f32),
+            pltpu.VMEM((count_r - 1, size_r, LANES), f32),
+            pltpu.VMEM((size_e, LANES), f32),
+            pltpu.VMEM((size_e, LANES), f32),
+            pltpu.VMEM(sums.shape, f32),
+            pltpu.SemaphoreType.DMA((copies,)),
+            pltpu.SemaphoreType.DMA((copies,)),
+        ],
+        compiler_params=pltpu.CompilerParams(collective_id=0, has_side_effects=True),
+    )(sums)
+    return tuple(out.reshape(item.shape) for out, item in zip(outs, weights))
 
 
 def on_device(pixels, feature_grad, tissue_count, *weights):
-    features, totals = encode_slots(pixels, feature_grad, tissue_count, weights)
-    shapes = [item.shape for item in totals]
-    flat = jnp.concatenate([item.reshape(-1) for item in totals])
-    flat = lax.psum(flat, ("region", "enc"))
-    summed = []
-    at = 0
-    for shape in shapes:
-        size = int(np.prod(shape))
-        summed.append(flat[at : at + size].reshape(shape))
-        at += size
-    return (features, *summed)
+    share = lax.axis_size("enc") * lax.axis_size("region")
+    features, sums = encode_slots(pixels, feature_grad, tissue_count, weights, share)
+    return (features, *summed_over_devices(sums, weights))
 
 
 def solution(mesh):

time: 403 us -> 222 us (0.55)
  waiting for transfers between devices: 195 us -> 0 us
  Pallas kernels: 156 us -> 202 us
  between operations: 14.9 us -> 1.3 us
  local copies, waits for them, and re-layouts: 29.3 us -> 16.6 us
  matrix products: 4.91 us -> 0 us
    psum x1 -> x0, waiting for transfers between devices: 195 us -> none  [on_device(): flat = lax.psum(flat, ('region', 'enc'))]
    pallas_call x0 -> x1, Pallas kernels: none -> 108 us  [summed_over_devices(): pl.pallas_call(add_up, in_specs=[pl.BlockSpec(memory_space=pltpu.VMEM)],...]
    pallas_call x1, Pallas kernels: 156 us -> 94 us  [encode_slots(): pl.pallas_call(body, grid_spec=pltpu.PrefetchScalarGridSpec(num_scalar_pr...]
    concatenate x2 -> x0, local copies, waits for them, and re-layouts: 8.26 us -> none  [the longest x1 7.39 us: on_device(): flat = jnp.concatenate([item.reshape(-1) for item in totals])]
    slice x7 -> x0, local copies, waits for them, and re-layouts: 7.66 us -> none  [the longest x5 5.13 us: on_device(): summed.append(flat[at:at + size].reshape(shape))]
    unnamed x20 -> x11, local copies, waits for them, and re-layouts: 8.28 us -> 15.3 us
    dot_general x3 -> x0, matrix products: 4.91 us -> none  [the longest x1 1.85 us: encode_slots(): jnp.dot(kernel[:, ::-1], place, precision=exact)]
  transfers between devices with their start and end apart: 1 -> 0, of which waited for: 1 -> 0; matrix products, arithmetic and copies ran while one was open for 0% -> 0% of each run, Pallas kernels for 0% -> 0%
where the time goes in v1:
time: 222 us; the launch traced here: 221 us
  Pallas kernels  202 us (91%)
  local copies, waits for them, and re-layouts  16.6 us (7%)
    pallas_call x1, Pallas kernels, summed_over_devices(): pl.pallas_call(add_up, in_specs=[pl.BlockSpec(memory_space=pltpu.VMEM)],...  108 us
    pallas_call x1, Pallas kernels, encode_slots(): pl.pallas_call(body, grid_spec=pltpu.PrefetchScalarGridSpec(num_scalar_pr...  94 us
    unnamed x11, local copies, waits for them, and re-layouts  15.3 us

profile of v1, /device:TPU:1, one launch (start us, length us, event | category | flops | bytes accessed | tf_op | source)
XLA Modules:
  0.0 221.0 jit_solution(11696946393423460577)
XLA Ops:
  1.3 1.2 broadcast_in_dim.19.bias_ref
  2.5 1.4 copy.25.ws_ref
  3.9 1.5 copy.26.kernel_ref
  5.4 1.6 copy.27.we_in_ref
  7.0 94.0 %shard_map.222 = (bf16[8,96,4096]{2,1,0:T(8,128)(2,1)}, f32[768,128]{1,0:T(8,128)}) custom-call(s32[1]{0:T(128)S(6)} %copy.36.count_ref, bf16[8,48,4096]{2,1,0:T(8,128)(2,1)} %pix_ref.1, bf16[8,96,4096]{2,1,0:T(8,128)(2,1)} %grad_ref.1, bf16[96,48]{1,0:T(8,128)(2,1)} %copy.25.ws_ref, f32[1,96]{1,0:T(1,128)} %bitcast.8, f32[1,96]{1,0:T(1,128)} %bitcast.9, ...), custom_call_target="tpu_custom_call" | custom-call | tf_op jit(solution)/shard_map/pallas_call | solution.py:323
  101.1 107.8 %shard_map.223 = (f32[96,48]{1,0:T(8,128)}, f32[1,96]{1,0:T(1,128)}, f32[1,96]{1,0:T(1,128)}, f32[96,49]{1,0:T(8,128)}, f32[1,96]{1,0:T(1,128)}, /*index=5*/f32[...) custom-call(f32[768,128]{1,0:T(8,128)} %get-tuple-element.22.sums_ref), custom_call_target="tpu_custom_call" | custom-call | tf_op jit(solution)/shard_map/pallas_call | solution.py:450
  208.9 1.5 copy.28
  210.4 1.3 reduce
  211.6 1.5 copy.29
  213.1 1.7 copy.30
  214.8 1.1 copy.37
  216.0 1.2 copy.38
  217.1 1.1 copy.39
  218.2 1.6 copy.40
  219.8 1.2 copy.41
